TPU v7x, 256 devices: a whole 4x4x8 slice. The times are simulated.
256 devices in a mesh: dp: 16 (over x_lo, y, core), mp: 8 (over z), side: 2 (over x_hi).
Axes of the slice: x: 4 (x_hi: 2, x_lo: 2; x = x_hi * 2 + x_lo), y: 4, z: 8, core: 2. Of those that a mesh axis runs over, the one named last changes fastest.
Arguments:
- tokens: bfloat16 [4096, 3072], P('dp', 'mp'), may hold values from -6 to 6
- up_weight: bfloat16 [2, 3072, 6144], P('side', 'dp', 'mp'), may hold values from -0.109375 to 0.109375
- down_weight: bfloat16 [2, 6144, 3072], P('side', 'mp', 'dp'), may hold values from -0.078125 to 0.078125
- mod_table: float32 [2, 50, 3, 3072], P('side'), may hold values from -3 to 3
- timesteps: int32 [16], P('dp'), may hold values from 0 to 49
- valid_counts: int32 [16], replicated, may hold values from 64 to 256, as said below
Outputs:
- block_out: bfloat16 [2, 4096, 3072], P('side', 'dp', 'mp')
- up_grads: float32 [3072, 6144], P(('dp', 'side'), 'mp')
- down_grads: float32 [6144, 3072], P('mp', ('dp', 'side'))
Inputs may be any that keep to these rules, and one draw needn't show every extreme that they name: `valid_counts`: every image has at least 64 valid tokens, and in every draw some image has all 256 valid.
All inputs are finite; a program needn't handle non-finite values.
Results may differ from a plain program's by a relative error of at most 0.018.
Values may be sent and summed in bfloat16 or wider, within the bound.
A program may use at most 64 MiB of HBM per device.

v0:
```python
import jax
import jax.numpy as jnp
from jax import lax
from jax.sharding import PartitionSpec as P


def passed_along(x, axis, by):
    peers = lax.axis_size(axis)
    pairs = [(i, i + by) for i in range(peers) if 0 <= i + by < peers]
    return lax.ppermute(x, axis, pairs)


def gelu_tanh(values):
    return jax.nn.gelu(values, approximate=True)


def shards(tokens, up_weight, down_weight, mod_table, timesteps, valid_counts):
    gathered = lax.all_gather(tokens, "mp", axis=1, tiled=True)
    width = gathered.shape[1]
    shard_width = tokens.shape[1]
    mp_offset = lax.axis_index("mp") * shard_width
    is_student = lax.axis_index("side") == 1
    wide = gathered.astype(jnp.float32)
    average = jnp.mean(wide, axis=-1, keepdims=True)
    centred = wide - average
    variance = jnp.mean(centred * centred, axis=-1, keepdims=True)
    scaled = centred * lax.rsqrt(variance + 1e-06)
    plan = mod_table.shape[1]
    one_hot = (jnp.arange(plan, dtype=jnp.int32)[None, :] == timesteps[0]).astype(jnp.float32)
    modulation = jnp.dot(
        one_hot,
        mod_table[0].reshape(plan, 3 * width),
        precision=lax.Precision.HIGHEST,
        preferred_element_type=jnp.float32,
    ).reshape(3, width)
    normed = (scaled * (1.0 + modulation[1]) + modulation[0]).astype(jnp.bfloat16)
    gate_row = modulation[2]
    hidden_pre = jnp.dot(
        normed,
        lax.all_gather(up_weight[0], "dp", axis=0, tiled=True),
        preferred_element_type=jnp.float32,
    )
    hidden_act = gelu_tanh(hidden_pre).astype(jnp.bfloat16)
    down_full = lax.all_gather(down_weight[0], "dp", axis=1, tiled=True)
    partial_value = jnp.dot(hidden_act, down_full, preferred_element_type=jnp.float32)
    positions = jnp.arange(normed.shape[0], dtype=jnp.int32)
    own_count = lax.dynamic_index_in_dim(valid_counts, lax.axis_index("dp"), 0, keepdims=False)
    valid_col = (positions < own_count).astype(jnp.float32)[:, None]
    valid_total = jnp.sum(valid_counts).astype(jnp.float32)
    mixed = lax.psum(partial_value.astype(jnp.bfloat16), "mp").astype(jnp.float32)
    out_full = (wide + gate_row * mixed).astype(jnp.bfloat16)
    out_local = lax.dynamic_slice_in_dim(out_full, mp_offset, shard_width, 1)
    other_full = passed_along(out_full, "side", 1)
    differ = out_full.astype(jnp.float32) - other_full.astype(jnp.float32)
    grad_out = (gate_row * differ * valid_col / jnp.sqrt(valid_total)).astype(jnp.bfloat16)

    def backprop():
        grad_act = lax.dot_general(
            grad_out, down_full, (((1,), (1,)), ((), ())), preferred_element_type=jnp.float32
        )
        unused, pullback = jax.vjp(gelu_tanh, hidden_pre)
        return pullback(grad_act)[0].astype(jnp.bfloat16)

    def no_backprop():
        return jnp.zeros(hidden_pre.shape, jnp.bfloat16)

    grad_pre = lax.cond(is_student, backprop, no_backprop)
    ff_width = hidden_act.shape[1]

    def product():
        return lax.dot_general(
            normed, grad_pre, (((0,), (0,)), ((), ())), preferred_element_type=jnp.float32
        )

    def nothing():
        return jnp.zeros(
            (width // lax.axis_size(("dp", "side")) * lax.axis_size(("dp", "side")), ff_width),
            jnp.float32,
        )

    up_share = lax.psum_scatter(
        lax.cond(is_student, product, nothing).astype(jnp.bfloat16),
        ("dp", "side"),
        scatter_dimension=0,
        tiled=True,
    ).astype(jnp.float32)

    def down_product():
        return lax.dot_general(
            hidden_act, grad_out, (((0,), (0,)), ((), ())), preferred_element_type=jnp.float32
        )

    def down_nothing():
        return jnp.zeros((ff_width, width), jnp.float32)

    down_term = lax.cond(is_student, down_product, down_nothing)
    down_share = lax.psum_scatter(
        down_term.astype(jnp.bfloat16), ("dp", "side"), scatter_dimension=1, tiled=True
    ).astype(jnp.float32)
    return (out_local[None], up_share, down_share)


def solution(mesh):
    placed = (
        P("dp", "mp"),
        P("side", "dp", "mp"),
        P("side", "mp", "dp"),
        P("side", None, None, None),
        P("dp"),
        P(),
    )
    return jax.shard_map(
        shards,
        mesh=mesh,
        in_specs=placed,
        out_specs=(P("side", "dp", "mp"), P(("dp", "side"), "mp"), P("mp", ("dp", "side"))),
        check_vma=False,
    )
```

profile of v0, /device:TPU:1, one launch (start us, length us, event | category | flops | bytes accessed | tf_op | source)
XLA Modules:
  0.0 593.4 jit_solution(2284106600337096998)
XLA Ops:
  7.2 0.0 all-gather.6.cloned.1.call-start
  7.2 0.7 all-gather.6.cloned.1.call-update
  7.9 0.0 all-gather.8.cloned.1.call-start
  7.9 0.7 all-gather.8.cloned.1.call-update
  8.6 0.0 all-gather.10.cloned.1.call-start
  8.7 0.7 all-gather.10.cloned.1.call-update
  9.4 0.0 all-reduce.2.cloned.1.call-start
  9.4 6.5 %reduce = f32[50,3,3072]{2,1,0:T(4,128)S(1)} reduce(f32[1,50,3,3072]{3,0,2,1:T(1,128)} %param.15, f32[]{:T(128)} %constant.65), dimensions={0}, to_apply=%param.15.reduce_sub_computation | reduce | bytes 3686404 | tf_op args[3]
  15.9 0.5 pad
  16.5 1.2 copy.14
  18.3 0.8 fusion.24
  19.1 29.2 %all-gather.6.cloned.1.call-done = bf16[256,3072]{1,0:T(8,128)(2,1)} async-done(((bf16[256,384]{1,0:T(8,128)(2,1)}), bf16[256,3072]{1,0:T(8,128)(2,1)}) %all-gather.6.cloned.1.call-update) | async-done | bytes 1572880 | tf_op jit(solution)/shard_map/all_gather | solution.py:18
  48.2 0.0 copy-start
  48.2 1.8 convert_reduce_fusion
  50.1 2.0 fusion.11
  52.0 0.0 copy-done
  52.0 0.8 fusion.14
  52.8 41.7 %all-gather.8.cloned.1.call-done = bf16[1,3072,768]{2,1,0:T(8,128)(2,1)} async-done(((bf16[1,192,768]{2,1,0:T(8,128)(2,1)}), bf16[1,3072,768]{2,1,0:T(8,128)(2,1)}) %all-gather.8.cloned.1.call-update) | async-done | bytes 4718608 | tf_op jit(solution)/shard_map/all_gather | solution.py:40
  94.5 4.6 fusion.23
  99.2 0.0 copy-start.1
  99.2 37.7 %all-gather.10.cloned.1.call-done = bf16[1,768,3072]{1,2,0:T(8,128)(2,1)} async-done(((bf16[1,768,192]{1,2,0:T(8,128)(2,1)}), bf16[1,768,3072]{1,2,0:T(8,128)(2,1)}) %all-gather.10.cloned.1.call-update) | async-done | bytes 4718608 | tf_op jit(solution)/shard_map/all_gather | solution.py:44
  136.9 4.9 convolution_convert_fusion
  141.8 0.0 copy-done.1
  141.8 0.0 copy-start.3
  141.8 0.0 all-reduce.2.cloned.1.call-update
  141.8 0.2 reduce-scatter.3.cloned.1.call-start
  142.1 74.3 %all-reduce.2.cloned.1.call-done = bf16[256,3072]{1,0:T(8,128)(2,1)} async-done(((bf16[256,3072]{1,0:T(8,128)(2,1)}), bf16[256,3072]{1,0:T(8,128)(2,1)}) %all-reduce.2.cloned.1.call-update) | async-done | bytes 1572880 | tf_op jit(solution)/shard_map/psum | solution.py:50
  216.3 3.1 fusion.15
  219.5 5.8 collective-permute-start
  225.2 0.0 copy-done.3
  225.2 0.6 reduce_sum.29
  226.6 0.6 dynamic_slice.8
  227.2 0.6 compare_convert_fusion
  227.8 25.6 %collective-permute-done = bf16[256,3072]{1,0:T(8,128)(2,1)} collective-permute-done((bf16[256,3072]{1,0:T(8,128)(2,1)}, bf16[256,3072]{1,0:T(8,128)(2,1)}, u32[]{:S(2)}, u32[]{:S(2)}) %collective-permute-start) | collective-permute-done | bytes 1572896 | tf_op jit(solution)/shard_map/ppermute | solution.py:10
  253.4 2.6 divide_convert_fusion
  256.0 0.1 conditional.3
  256.1 2.5 conditional.4
  256.1 2.5 broadcast.75
  258.6 0.0 copy-start.2
  258.6 0.0 reduce-scatter.3.cloned.1.call-update
  258.6 0.0 reduce-scatter.5.cloned.1.call-start
  258.6 0.9 copy-done.2
  259.6 2.8 conditional.5
  259.6 2.8 broadcast.76
  262.4 6.6 %copy.12 = bf16[768,3072]{0,1:T(8,128)(2,1)} copy(bf16[768,3072]{1,0:T(8,128)(2,1)} %get-tuple-element.43) | data formatting | bytes 9437184 | tf_op jit(solution)/shard_map/cond | solution.py:96
  269.0 0.0 reduce-scatter.5.cloned.1.call-update
  269.0 1.6 dynamic-slice_bitcast_fusion
  270.6 155.2 %reduce-scatter.3.cloned.1.call-done = bf16[96,768]{1,0:T(8,128)(2,1)} async-done(((bf16[3072,768]{1,0:T(8,128)(2,1)}), bf16[96,768]{1,0:T(8,128)(2,1)}) %reduce-scatter.3.cloned.1.call-update) | async-done | bytes 147472 | tf_op jit(solution)/shard_map/reduce_scatter | solution.py:81
  425.9 1.6 convert_element_type.71
  427.5 157.4 %reduce-scatter.5.cloned.1.call-done = bf16[768,96]{0,1:T(8,128)(2,1)} async-done(((bf16[768,3072]{0,1:T(8,128)(2,1)}), bf16[768,96]{0,1:T(8,128)(2,1)}) %reduce-scatter.5.cloned.1.call-update) | async-done | bytes 147472 | tf_op jit(solution)/shard_map/reduce_scatter | solution.py:97
  584.9 1.6 convert_element_type.73
  (4 shorter events, 0.1 us)
Async XLA Ops:
  7.2 41.1 %all-gather.6.cloned.1.call-start = ((), (), s32[]{:S(2)}) async-start(), calls=%async_computation.2 | async-start | bytes 1769472 | tf_op jit(solution)/shard_map/all_gather | solution.py:18
  7.9 86.6 %all-gather.8.cloned.1.call-start = ((), (), s32[]{:S(2)}) async-start(), calls=%async_computation.6 | async-start | bytes 5013504 | tf_op jit(solution)/shard_map/all_gather | solution.py:40
  8.6 128.2 %all-gather.10.cloned.1.call-start = ((), (), s32[]{:S(2)}) async-start(), calls=%async_computation.7 | async-start | bytes 5013504 | tf_op jit(solution)/shard_map/all_gather | solution.py:44
  9.4 207.0 %all-reduce.2.cloned.1.call-start = ((), (), s32[]{:S(2)}) async-start(), calls=%async_computation.3 | async-start | bytes 3145728 | tf_op jit(solution)/shard_map/psum | solution.py:50
  48.2 3.8 copy-start
  99.2 42.7 %copy-start.1 = (bf16[256,768]{1,0:T(8,128)(2,1)}, bf16[256,768]{1,0:T(8,128)(2,1)S(1)}, u32[]{:S(2)}) copy-start(bf16[256,768]{1,0:T(8,128)(2,1)S(1)} %get-tuple-element.39) | copy-start | bytes 1179652
  141.8 83.4 %copy-start.3 = (s32[16]{0:T(128)S(1)}, s32[16]{0:T(128)}, u32[]{:S(2)}) copy-start(s32[16]{0:T(128)} %param.17) | copy-start | bytes 196
  141.8 284.0 %reduce-scatter.3.cloned.1.call-start = ((), (), s32[]{:S(2)}) async-start(), calls=%async_computation.4 | async-start | bytes 4866048 | tf_op jit(solution)/shard_map/reduce_scatter | solution.py:81
  219.5 34.0 %collective-permute-start = (bf16[256,3072]{1,0:T(8,128)(2,1)}, bf16[256,3072]{1,0:T(8,128)(2,1)}, u32[]{:S(2)}, u32[]{:S(2)}) collective-permute-start(bf16[256,3072]{1,0:T(8,128)(2,1)} %fusion.15), channel_id=1, source_target_pairs={{0,1},{2,3},{4,5},{6,7},{8,9},{10,11},{12,13},{14,15},{16,17},{18,... | collective-permute-start | bytes 4718600 | tf_op jit(solution)/shard_map/ppermute | solution.py:10
  258.6 1.0 copy-start.2
  258.6 326.3 %reduce-scatter.5.cloned.1.call-start = ((), (), s32[]{:S(2)}) async-start(), calls=%async_computation.5 | async-start | bytes 4866048 | tf_op jit(solution)/shard_map/reduce_scatter | solution.py:97
Sparse Core Ops, SparseCore 0:
  9.8 38.4 all-gather.5
  50.1 44.3 all-gather.7
  96.4 40.4 all-gather.9
  142.0 74.3 all-reduce.1
  258.7 167.0 reduce-scatter.2
  428.2 156.6 reduce-scatter.4
where the time goes:
time: 594 us; the launch traced here: 593 us
  waiting for transfers between devices  523 us (88%)
  other arithmetic  21.3 us (4%)
  local copies, waits for them, and re-layouts  16.8 us (3%)
  between operations  15.5 us (3%)
  matrix products  10.3 us (2%)
  starting transfers between devices  6.19 us (1%)
    reduce_scatter x1, waiting for transfers between devices, shards(): lax.psum_scatter(down_term.astype(jnp.bfloat16), ('dp', 'side'), scatter_...  157 us
    reduce_scatter x1, waiting for transfers between devices, shards(): lax.psum_scatter(lax.cond(is_student, product, nothing).astype(jnp.bfloat...  155 us
    psum x1, waiting for transfers between devices, shards(): lax.psum(partial_value.astype(jnp.bfloat16), 'mp').astype(jnp.float32)  74.3 us
    all_gather x1, waiting for transfers between devices, shards(): lax.all_gather(up_weight[0], 'dp', axis=0, tiled=True)  41.7 us
    all_gather x1, waiting for transfers between devices, shards(): down_full = lax.all_gather(down_weight[0], 'dp', axis=1, tiled=True)  37.7 us
    all_gather x1, waiting for transfers between devices, shards(): gathered = lax.all_gather(tokens, 'mp', axis=1, tiled=True)  29.2 us
    ppermute x1, waiting for transfers between devices, passed_along(): return lax.ppermute(x, axis, pairs)  25.6 us
  transfers between devices with their start and end apart: 7, of which 7 were waited for; matrix products, arithmetic and copies ran while one was open for 6% of the time, Pallas kernels for 0%

commit v1 on v0

--- a/solution.py
+++ b/solution.py
@@ -41,7 +41,9 @@
         preferred_element_type=jnp.float32,
     )
     hidden_act = gelu_tanh(hidden_pre).astype(jnp.bfloat16)
-    down_full = lax.all_gather(down_weight[0], "dp", axis=1, tiled=True)
+    down_full = jnp.concatenate(
+        lax.all_to_all(jnp.stack([down_weight[0]] * lax.axis_size("dp")), "dp", 0, 0), axis=1
+    )
     partial_value = jnp.dot(hidden_act, down_full, preferred_element_type=jnp.float32)
     positions = jnp.arange(normed.shape[0], dtype=jnp.int32)
     own_count = lax.dynamic_index_in_dim(valid_counts, lax.axis_index("dp"), 0, keepdims=False)

time: 594 us -> 573 us (0.965)
  waiting for transfers between devices: 523 us -> 492 us
  starting transfers between devices: 6.19 us -> 13.6 us
    all_gather x1 -> x0, waiting for transfers between devices: 37.7 us -> none  [shards(): down_full = lax.all_gather(down_weight[0], 'dp', axis=1, tiled=True)]
    all_gather x1, waiting for transfers between devices: 41.7 us -> 53.2 us  [shards(): lax.all_gather(up_weight[0], 'dp', axis=0, tiled=True)]
    all_gather x1, waiting for transfers between devices: 29.2 us -> 19.7 us  [shards(): gathered = lax.all_gather(tokens, 'mp', axis=1, tiled=True)]
    all_to_all x0 -> x1, starting transfers between devices: none -> 7.5 us  [shards(): lax.all_to_all(jnp.stack([down_weight[0]] * lax.axis_size('dp')), 'dp', 0...]
  transfers between devices with their start and end apart: 7 -> 7, of which waited for: 7 -> 6; matrix products, arithmetic and copies ran while one was open for 6% -> 6% of each run, Pallas kernels for 0% -> 0%
where the time goes in v1:
time: 573 us
  waiting for transfers between devices  492 us (86%)
  other arithmetic  21.3 us (4%)
  local copies, waits for them, and re-layouts  20.4 us (4%)
  between operations  15.2 us (3%)
  starting transfers between devices  13.6 us (2%)
  matrix products  10.5 us (2%)
    reduce_scatter x1, waiting for transfers between devices, shards(): lax.psum_scatter(down_term.astype(jnp.bfloat16), ('dp', 'side'), scatter_...  161 us
    reduce_scatter x1, waiting for transfers between devices, shards(): lax.psum_scatter(lax.cond(is_student, product, nothing).astype(jnp.bfloat...  155 us
    psum x1, waiting for transfers between devices, shards(): lax.psum(partial_value.astype(jnp.bfloat16), 'mp').astype(jnp.float32)  75.7 us
    all_gather x1, waiting for transfers between devices, shards(): lax.all_gather(up_weight[0], 'dp', axis=0, tiled=True)  53.2 us
    ppermute x1, waiting for transfers between devices, passed_along(): return lax.ppermute(x, axis, pairs)  25.6 us
    all_gather x1, waiting for transfers between devices, shards(): gathered = lax.all_gather(tokens, 'mp', axis=1, tiled=True)  19.7 us
  transfers between devices with their start and end apart: 7, of which 6 were waited for; matrix products, arithmetic and copies ran while one was open for 6% of the time, Pallas kernels for 0%

profile of v1, /device:TPU:1, one launch (start us, length us, event | category | flops | bytes accessed | tf_op | source)
XLA Modules:
  0.0 572.6 jit_solution(12400570121871779215)
XLA Ops:
  7.2 0.0 all-gather.4.cloned.1.call-start
  7.2 0.7 all-gather.4.cloned.1.call-update
  7.9 0.0 all-gather.6.cloned.1.call-start
  7.9 0.7 all-gather.6.cloned.1.call-update
  8.6 3.6 stack.3
  12.2 7.5 %all-to-all-start = ((bf16[16,768,192]{1,2,0:T(8,128)(2,1)}), bf16[16,768,192]{1,2,0:T(8,128)(2,1)}, u32[]{:S(2)}, u32[]{:S(2)}) async-start(bf16[16,768,192]{1,2,0:T(8,128)(2,1)} %stack.3), calls=%async_computation | async-start | bytes 9437184 | tf_op jit(solution)/shard_map/all_to_all | solution.py:45
  19.7 0.0 all-reduce.2.cloned.1.call-start
  19.8 6.5 %reduce = f32[50,3,3072]{2,1,0:T(4,128)S(1)} reduce(f32[1,50,3,3072]{3,0,2,1:T(1,128)} %param.15, f32[]{:T(128)} %constant.65), dimensions={0}, to_apply=%param.15.reduce_sub_computation | reduce | bytes 3686404 | tf_op args[3]
  26.3 0.5 pad
  26.8 1.2 copy.14
  28.6 0.8 fusion.24
  29.4 19.7 %all-gather.4.cloned.1.call-done = bf16[256,3072]{1,0:T(8,128)(2,1)} async-done(((bf16[256,384]{1,0:T(8,128)(2,1)}), bf16[256,3072]{1,0:T(8,128)(2,1)}) %all-gather.4.cloned.1.call-update) | async-done | bytes 1572880 | tf_op jit(solution)/shard_map/all_gather | solution.py:18
  49.2 0.0 copy-start
  49.2 1.8 convert_reduce_fusion
  51.0 2.0 fusion.11
  53.0 0.0 copy-done
  53.0 0.8 fusion.14
  53.8 53.2 %all-gather.6.cloned.1.call-done = bf16[1,3072,768]{2,1,0:T(8,128)(2,1)} async-done(((bf16[1,192,768]{2,1,0:T(8,128)(2,1)}), bf16[1,3072,768]{2,1,0:T(8,128)(2,1)}) %all-gather.6.cloned.1.call-update) | async-done | bytes 4718608 | tf_op jit(solution)/shard_map/all_gather | solution.py:40
  107.0 4.6 fusion.23
  111.7 0.0 copy-start.1
  111.7 0.0 all-to-all-done
  111.7 5.0 convolution_convert_fusion
  116.7 0.0 copy-done.1
  116.7 0.0 copy-start.3
  116.7 0.0 all-reduce.2.cloned.1.call-update
  116.7 0.2 reduce-scatter.3.cloned.1.call-start
  117.0 75.7 %all-reduce.2.cloned.1.call-done = bf16[256,3072]{1,0:T(8,128)(2,1)} async-done(((bf16[256,3072]{1,0:T(8,128)(2,1)}), bf16[256,3072]{1,0:T(8,128)(2,1)}) %all-reduce.2.cloned.1.call-update) | async-done | bytes 1572880 | tf_op jit(solution)/shard_map/psum | solution.py:52
  192.7 3.1 fusion.15
  195.8 5.8 %collective-permute-start = (bf16[256,3072]{1,0:T(8,128)(2,1)}, bf16[256,3072]{1,0:T(8,128)(2,1)}, u32[]{:S(2)}, u32[]{:S(2)}) collective-permute-start(bf16[256,3072]{1,0:T(8,128)(2,1)} %fusion.15), channel_id=1, source_target_pairs={{0,1},{2,3},{4,5},{6,7},{8,9},{10,11},{12,13},{14,15},{16,17},{18,... | collective-permute-start | bytes 4718600 | tf_op jit(solution)/shard_map/ppermute | solution.py:10
  201.6 0.0 copy-done.3
  201.6 0.6 reduce_sum.29
  202.9 0.6 dynamic_slice.8
  203.5 0.6 compare_convert_fusion
  204.1 25.6 %collective-permute-done = bf16[256,3072]{1,0:T(8,128)(2,1)} collective-permute-done((bf16[256,3072]{1,0:T(8,128)(2,1)}, bf16[256,3072]{1,0:T(8,128)(2,1)}, u32[]{:S(2)}, u32[]{:S(2)}) %collective-permute-start) | collective-permute-done | bytes 1572896 | tf_op jit(solution)/shard_map/ppermute | solution.py:10
  229.8 2.6 divide_convert_fusion
  232.3 0.1 conditional.3
  232.4 2.5 conditional.4
  232.4 2.5 broadcast.76
  234.9 0.0 copy-start.2
  234.9 0.0 reduce-scatter.3.cloned.1.call-update
  234.9 0.0 reduce-scatter.5.cloned.1.call-start
  235.0 0.9 copy-done.2
  235.9 2.8 conditional.5
  235.9 2.8 broadcast.77
  238.7 6.6 %copy.12 = bf16[768,3072]{0,1:T(8,128)(2,1)} copy(bf16[768,3072]{1,0:T(8,128)(2,1)} %get-tuple-element.43) | data formatting | bytes 9437184 | tf_op jit(solution)/shard_map/cond | solution.py:98
  245.3 0.0 reduce-scatter.5.cloned.1.call-update
  245.3 1.6 dynamic-slice_bitcast_fusion
  247.0 154.6 %reduce-scatter.3.cloned.1.call-done = bf16[96,768]{1,0:T(8,128)(2,1)} async-done(((bf16[3072,768]{1,0:T(8,128)(2,1)}), bf16[96,768]{1,0:T(8,128)(2,1)}) %reduce-scatter.3.cloned.1.call-update) | async-done | bytes 147472 | tf_op jit(solution)/shard_map/reduce_scatter | solution.py:83
  401.5 1.6 convert_element_type.71
  403.2 161.3 %reduce-scatter.5.cloned.1.call-done = bf16[768,96]{0,1:T(8,128)(2,1)} async-done(((bf16[768,3072]{0,1:T(8,128)(2,1)}), bf16[768,96]{0,1:T(8,128)(2,1)}) %reduce-scatter.5.cloned.1.call-update) | async-done | bytes 147472 | tf_op jit(solution)/shard_map/reduce_scatter | solution.py:99
  564.5 1.6 convert_element_type.73
  (4 shorter events, 0.1 us)
Async XLA Ops:
  7.2 42.0 %all-gather.4.cloned.1.call-start = ((), (), s32[]{:S(2)}) async-start(), calls=%async_computation.3 | async-start | bytes 1769472 | tf_op jit(solution)/shard_map/all_gather | solution.py:18
  7.9 99.1 %all-gather.6.cloned.1.call-start = ((), (), s32[]{:S(2)}) async-start(), calls=%async_computation.7 | async-start | bytes 5013504 | tf_op jit(solution)/shard_map/all_gather | solution.py:40
  12.2 99.4 %all-to-all-start = ((bf16[16,768,192]{1,2,0:T(8,128)(2,1)}), bf16[16,768,192]{1,2,0:T(8,128)(2,1)}, u32[]{:S(2)}, u32[]{:S(2)}) async-start(bf16[16,768,192]{1,2,0:T(8,128)(2,1)} %stack.3), calls=%async_computation | async-start | bytes 9437184 | tf_op jit(solution)/shard_map/all_to_all | solution.py:45
  19.7 172.9 %all-reduce.2.cloned.1.call-start = ((), (), s32[]{:S(2)}) async-start(), calls=%async_computation.4 | async-start | bytes 3145728 | tf_op jit(solution)/shard_map/psum | solution.py:52
  49.2 3.8 copy-start
  111.7 5.1 copy-start.1
  116.7 84.9 %copy-start.3 = (s32[16]{0:T(128)S(1)}, s32[16]{0:T(128)}, u32[]{:S(2)}) copy-start(s32[16]{0:T(128)} %param.17) | copy-start | bytes 196
  116.7 284.8 %reduce-scatter.3.cloned.1.call-start = ((), (), s32[]{:S(2)}) async-start(), calls=%async_computation.5 | async-start | bytes 4866048 | tf_op jit(solution)/shard_map/reduce_scatter | solution.py:83
  195.8 34.0 %collective-permute-start = (bf16[256,3072]{1,0:T(8,128)(2,1)}, bf16[256,3072]{1,0:T(8,128)(2,1)}, u32[]{:S(2)}, u32[]{:S(2)}) collective-permute-start(bf16[256,3072]{1,0:T(8,128)(2,1)} %fusion.15), channel_id=1, source_target_pairs={{0,1},{2,3},{4,5},{6,7},{8,9},{10,11},{12,13},{14,15},{16,17},{18,... | collective-permute-start | bytes 4718600 | tf_op jit(solution)/shard_map/ppermute | solution.py:10
  234.9 1.0 copy-start.2
  234.9 329.6 %reduce-scatter.5.cloned.1.call-start = ((), (), s32[]{:S(2)}) async-start(), calls=%async_computation.6 | async-start | bytes 4866048 | tf_op jit(solution)/shard_map/reduce_scatter | solution.py:99
Sparse Core Ops, SparseCore 0:
  9.8 39.3 all-gather.3
  51.0 55.9 all-gather.5
  116.9 75.7 all-reduce.1
  235.0 166.4 reduce-scatter.2
  403.9 160.5 reduce-scatter.4
